TPU v7x, 32 devices: a whole 2x2x4 slice. The times are simulated.
32 devices in a mesh: energy: 8 (over y, x, core), slab: 4 (over z).
Axes of the slice: x: 2, y: 2, z: 4, core: 2. Of those that a mesh axis runs over, the one named last changes fastest.
Arguments:
- green: bfloat16 [32, 8, 2, 128, 128], P('energy', 'slab'), may hold values from -6 to 6
- coupling: bfloat16 [8, 6, 2, 128, 128], P('slab'), may hold values from -0.1875 to 0.1875
- neighbours: int32 [8, 6], P('slab'), may hold values from 0 to 7, as said below
- shifts: int32 [2], replicated, may hold values from 1 to 4, as said below
- occupation: float32 [2], replicated, may hold values from 0.3 to 3
Outputs:
- self_energy: bfloat16 [32, 8, 2, 128, 128], P('energy', 'slab')
Inputs may be any that keep to these rules, and one draw needn't show every extreme that they name: `neighbours`: each entry differs from its own atom's index by 1 to 2; column 0 differs by exactly 2. `shifts`: exactly one mode has shift 4; the others are below it.
All inputs are finite; a program needn't handle non-finite values.
Results may differ from a plain program's by a relative error of at most 0.0057.
Values may be sent and summed in bfloat16 or wider, within the bound.
A program may use at most 128 MiB of HBM per device.

v0:
```python
import jax
import jax.numpy as jnp
from jax import lax
from jax.sharding import PartitionSpec as P

WID = 4
HALO = 2


def with_halo(x, sides, width):
    for axis, dim in sides:
        count, length = (lax.axis_size(axis), x.shape[dim])
        up = [(i, (i + 1) % count) for i in range(count - 1)]
        down = [(j, i) for i, j in up]
        last = lax.slice_in_dim(x, length - width, length, axis=dim)
        first = lax.slice_in_dim(x, 0, width, axis=dim)
        before = lax.ppermute(last, axis, up)
        after = lax.ppermute(first, axis, down)
        x = jnp.concatenate([before, x, after], axis=dim)
    return x


def mode_products(extended, coupling, local_index):
    atom_blocks = []
    for which_atom in range(coupling.shape[0]):
        per_mode = []
        for which_mode in range(coupling.shape[2]):
            running = jnp.zeros(
                (extended.shape[0], 2, extended.shape[3], extended.shape[4]), jnp.float32
            )
            for which_slot in range(coupling.shape[1]):
                source = lax.dynamic_index_in_dim(
                    extended, local_index[which_atom, which_slot], 1, keepdims=False
                )
                matrix = coupling[which_atom, which_slot, which_mode]
                half_product = jnp.einsum(
                    "ik,erkl->eril", matrix, source, preferred_element_type=jnp.float32
                ).astype(jnp.bfloat16)
                running = running + jnp.einsum(
                    "eril,jl->erij", half_product, matrix, preferred_element_type=jnp.float32
                )
            per_mode.append(running.astype(jnp.bfloat16))
        atom_blocks.append(jnp.stack(per_mode, 1))
    return jnp.stack(atom_blocks, 1)


def shards(green, coupling, neighbours, shifts, occupation):
    atom_count = green.shape[1]
    energies = green.shape[0]
    first_atom = lax.axis_index("slab") * atom_count
    local_index = neighbours - first_atom + HALO
    widened = with_halo(green, (("slab", 1),), HALO)
    local_products = mode_products(widened, coupling, local_index)
    products = with_halo(local_products, (("energy", 0),), WID)
    result = jnp.zeros((energies, atom_count, 2, green.shape[3], green.shape[4]), jnp.float32)
    for which_mode in range(coupling.shape[2]):
        mode_block = products[:, :, which_mode]
        step_size = shifts[which_mode]
        lower = lax.dynamic_slice_in_dim(mode_block, WID - step_size, energies, 0).astype(
            jnp.float32
        )
        upper = lax.dynamic_slice_in_dim(mode_block, WID + step_size, energies, 0).astype(
            jnp.float32
        )
        weight = occupation[which_mode]
        result = result + (weight + 1.0) * lower + weight * upper
    return result.astype(jnp.bfloat16)


def solution(mesh):
    placed = (
        P("energy", "slab", None, None, None),
        P("slab", None, None, None, None),
        P("slab", None),
        P(),
        P(),
    )
    return jax.shard_map(
        shards,
        mesh=mesh,
        in_specs=placed,
        out_specs=P("energy", "slab", None, None, None),
        check_vma=False,
    )
```

profile of v0, /device:TPU:1, one launch (start us, length us, event | category | flops | bytes accessed | tf_op | source)
XLA Modules:
  0.0 92.9 jit_solution(13113285735453428527)
XLA Ops:
  0.0 4.0 %collective-permute-start = (bf16[4,2,2,128,128]{4,3,2,1,0:T(8,128)(2,1)}, bf16[4,2,2,128,128]{4,3,2,1,0:T(8,128)(2,1)S(1)}, u32[]{:S(2)}, u32[]{:S(2)}) collective-permute-start(bf16[4,2,2,128,128]{4,3,2,1,0:T(8,128)(2,1)} %param.5), channel_id=1, source_target_pairs={{0,1},{1,2},{2,3},{4,5},{5,6},{6,7},{8,9},{9,10},{10,11},{12,13},{... | collective-permute-start | bytes 1572872 | tf_op jit(solution)/shard_map/ppermute | solution.py:17
  4.0 1.3 %collective-permute-start.1 = (bf16[4,2,2,128,128]{4,3,2,1,0:T(8,128)(2,1)}, bf16[4,2,2,128,128]{4,3,2,1,0:T(8,128)(2,1)S(1)}, u32[]{:S(2)}, u32[]{:S(2)}) collective-permute-start(bf16[4,2,2,128,128]{4,3,2,1,0:T(8,128)(2,1)} %param.5), channel_id=1, source_target_pairs={{1,0},{2,1},{3,2},{5,4},{6,5},{7,6},{9,8},{10,9},{11,10},{13,12},{... | collective-permute-start | bytes 1572872 | tf_op jit(solution)/shard_map/ppermute | solution.py:18
  5.4 0.7 subtract_add_fusion
  6.0 0.7 fusion.278
  29.3 0.0 copy-start
  29.3 0.0 collective-permute-done
  29.3 1.2 %constant_dynamic-update-slice_fusion.1 = bf16[4,6,2,128,128]{4,3,2,1,0:T(8,128)(2,1)S(1)} fusion(bf16[4,6,2,128,128]{4,3,2,1,0:T(8,128)(2,1)S(1)} %constant_dynamic-update-slice_fusion.2, bf16[4,2,2,128,128]{4,3,2,1,0:T(8,128)(2,1)} %param.5), kind=kLoop, calls=%fused_computation.183 | loop fusion | bytes 1048576
  30.5 0.0 collective-permute-done.1
  30.5 0.1 constant_dynamic-update-slice_fusion
  30.6 0.4 fusion.23
  31.0 1.2 %fusion.30 = f32[4,2,128,128]{3,2,1,0:T(8,128)} fusion(bf16[4,6,2,128,128]{4,3,2,1,0:T(8,128)(2,1)S(1)} %constant_dynamic-update-slice_fusion, s32[]{:T(128)S(6)} %select_n.67, bf16[2,6,2,128,128]{4,3,2,1,0:T(8,128)(2,1)S(1)} %copy-done), kind=kOutput, calls=%fused_computation.75 | convolution fusion | flops 67239936 | bytes 851972 | tf_op jit(solution)/shard_map/eril,jl->erij/dot_general | solution.py:39
  32.2 1.2 %fusion.9 = f32[4,2,128,128]{3,2,1,0:T(8,128)} fusion(bf16[4,6,2,128,128]{4,3,2,1,0:T(8,128)(2,1)S(1)} %constant_dynamic-update-slice_fusion, s32[]{:T(128)S(6)} %select_n.61, bf16[2,6,2,128,128]{4,3,2,1,0:T(8,128)(2,1)S(1)} %copy-done), kind=kOutput, calls=%fused_computation.54 | convolution fusion | flops 67239936 | bytes 851972 | tf_op jit(solution)/shard_map/eril,jl->erij/dot_general | solution.py:39
  33.4 1.2 %fusion.16 = f32[4,2,128,128]{3,2,1,0:T(8,128)} fusion(bf16[4,6,2,128,128]{4,3,2,1,0:T(8,128)(2,1)S(1)} %constant_dynamic-update-slice_fusion, s32[]{:T(128)S(6)} %select_n.61, bf16[2,6,2,128,128]{4,3,2,1,0:T(8,128)(2,1)S(1)} %copy-done), kind=kOutput, calls=%fused_computation.61 | convolution fusion | flops 67239936 | bytes 851972 | tf_op jit(solution)/shard_map/eril,jl->erij/dot_general | solution.py:39
  34.6 0.4 convolution_add_fusion.9
  35.0 1.4 %convolution_add_fusion.4 = f32[4,2,128,128]{3,2,1,0:T(8,128)S(1)} fusion(f32[4,2,128,128]{3,2,1,0:T(8,128)} %fusion.30, bf16[4,6,2,128,128]{4,3,2,1,0:T(8,128)(2,1)S(1)} %constant_dynamic-update-slice_fusion, s32[]{:T(128)S(6)} %select_n.68, bf16[2,6,2,128,128]{4,3,2,1,0:T(8,128)(2,1)S(1)} %copy-done), kind=kOutput, calls=%fused_computation.5 | convolution fusion | flops 67371008 | bytes 1376260 | tf_op jit(solution)/shard_map/eril,jl->erij/dot_general | solution.py:39
  36.4 1.2 %convolution_add_fusion.8 = f32[4,2,128,128]{3,2,1,0:T(8,128)} fusion(f32[4,2,128,128]{3,2,1,0:T(8,128)S(1)} %convolution_add_fusion.9, bf16[4,6,2,128,128]{4,3,2,1,0:T(8,128)(2,1)S(1)} %constant_dynamic-update-slice_fusion, s32[]{:T(128)S(6)} %select_n.69, bf16[2,6,2,128,128]{4,3,2,1,0:T(8,128)(2,1)S(1)} %copy-done), kind=kOutput, calls=%fused_computation.9 | convolution fusion | flops 67371008 | bytes 1376260 | tf_op jit(solution)/shard_map/eril,jl->erij/dot_general | solution.py:39
  37.6 0.4 convolution_add_fusion.3
  38.0 2.2 %convolution_add_fusion.7 = f32[4,2,128,128]{3,2,1,0:T(8,128)} fusion(f32[4,2,128,128]{3,2,1,0:T(8,128)} %convolution_add_fusion.8, bf16[4,6,2,128,128]{4,3,2,1,0:T(8,128)(2,1)S(1)} %constant_dynamic-update-slice_fusion, s32[]{:T(128)S(6)} %select_n.70, bf16[2,6,2,128,128]{4,3,2,1,0:T(8,128)(2,1)S(1)} %copy-done), kind=kOutput, calls=%fused_computation.8 | convolution fusion | flops 67371008 | bytes 1376260 | tf_op jit(solution)/shard_map/eril,jl->erij/dot_general | solution.py:39
  40.2 0.4 convolution_add_fusion.2
  40.6 2.2 %convolution_add_fusion.6 = f32[4,2,128,128]{3,2,1,0:T(8,128)} fusion(f32[4,2,128,128]{3,2,1,0:T(8,128)} %convolution_add_fusion.7, bf16[4,6,2,128,128]{4,3,2,1,0:T(8,128)(2,1)S(1)} %constant_dynamic-update-slice_fusion, s32[]{:T(128)S(6)} %select_n.71, bf16[2,6,2,128,128]{4,3,2,1,0:T(8,128)(2,1)S(1)} %copy-done), kind=kOutput, calls=%fused_computation.7 | convolution fusion | flops 67371008 | bytes 1376260 | tf_op jit(solution)/shard_map/eril,jl->erij/dot_general | solution.py:39
  42.9 0.4 convolution_add_fusion.1
  43.3 2.2 %fusion.5 = bf16[4,1,2,128,128]{4,3,2,0,1:T(8,128)(2,1)} fusion(f32[4,2,128,128]{3,2,1,0:T(8,128)} %convolution_add_fusion.6, bf16[4,6,2,128,128]{4,3,2,1,0:T(8,128)(2,1)S(1)} %constant_dynamic-update-slice_fusion, s32[]{:T(128)S(6)} %select_n.72, bf16[2,6,2,128,128]{4,3,2,1,0:T(8,128)(2,1)S(1)} %copy-done), kind=kOutput, calls=%fused_computation.50 | convolution fusion | flops 67502080 | bytes 1114116 | tf_op jit(solution)/shard_map/eril,jl->erij/dot_general | solution.py:39
  45.5 1.1 %fusion.4 = bf16[4,1,2,128,128]{4,3,2,0,1:T(8,128)(2,1)} fusion(f32[4,2,128,128]{3,2,1,0:T(8,128)S(1)} %convolution_add_fusion.1, bf16[4,6,2,128,128]{4,3,2,1,0:T(8,128)(2,1)S(1)} %constant_dynamic-update-slice_fusion, s32[]{:T(128)S(6)} %select_n.72, bf16[2,6,2,128,128]{4,3,2,1,0:T(8,128)(2,1)S(1)} %copy-done), kind=kOutput, calls=%fused_computation.49 | convolution fusion | flops 67502080 | bytes 1114116 | tf_op jit(solution)/shard_map/eril,jl->erij/dot_general | solution.py:39
  46.6 0.4 convolution_add_fusion.19
  47.0 1.4 %convolution_add_fusion.14 = f32[4,2,128,128]{3,2,1,0:T(8,128)S(1)} fusion(f32[4,2,128,128]{3,2,1,0:T(8,128)} %fusion.16, bf16[4,6,2,128,128]{4,3,2,1,0:T(8,128)(2,1)S(1)} %constant_dynamic-update-slice_fusion, s32[]{:T(128)S(6)} %select_n.62, bf16[2,6,2,128,128]{4,3,2,1,0:T(8,128)(2,1)S(1)} %copy-done), kind=kOutput, calls=%fused_computation.15 | convolution fusion | flops 67371008 | bytes 1376260 | tf_op jit(solution)/shard_map/eril,jl->erij/dot_general | solution.py:39
  48.4 1.2 %convolution_add_fusion.18 = f32[4,2,128,128]{3,2,1,0:T(8,128)} fusion(f32[4,2,128,128]{3,2,1,0:T(8,128)S(1)} %convolution_add_fusion.19, bf16[4,6,2,128,128]{4,3,2,1,0:T(8,128)(2,1)S(1)} %constant_dynamic-update-slice_fusion, s32[]{:T(128)S(6)} %select_n.63, bf16[2,6,2,128,128]{4,3,2,1,0:T(8,128)(2,1)S(1)} %copy-done), kind=kOutput, calls=%fused_computation.19 | convolution fusion | flops 67371008 | bytes 1376260 | tf_op jit(solution)/shard_map/eril,jl->erij/dot_general | solution.py:39
  49.6 0.4 convolution_add_fusion.13
  50.0 2.2 %convolution_add_fusion.17 = f32[4,2,128,128]{3,2,1,0:T(8,128)} fusion(f32[4,2,128,128]{3,2,1,0:T(8,128)} %convolution_add_fusion.18, bf16[4,6,2,128,128]{4,3,2,1,0:T(8,128)(2,1)S(1)} %constant_dynamic-update-slice_fusion, s32[]{:T(128)S(6)} %select_n.64, bf16[2,6,2,128,128]{4,3,2,1,0:T(8,128)(2,1)S(1)} %copy-done), kind=kOutput, calls=%fused_computation.18 | convolution fusion | flops 67371008 | bytes 1376260 | tf_op jit(solution)/shard_map/eril,jl->erij/dot_general | solution.py:39
  52.2 0.4 convolution_add_fusion.12
  52.6 2.2 %convolution_add_fusion.16 = f32[4,2,128,128]{3,2,1,0:T(8,128)} fusion(f32[4,2,128,128]{3,2,1,0:T(8,128)} %convolution_add_fusion.17, bf16[4,6,2,128,128]{4,3,2,1,0:T(8,128)(2,1)S(1)} %constant_dynamic-update-slice_fusion, s32[]{:T(128)S(6)} %select_n.65, bf16[2,6,2,128,128]{4,3,2,1,0:T(8,128)(2,1)S(1)} %copy-done), kind=kOutput, calls=%fused_computation.17 | convolution fusion | flops 67371008 | bytes 1376260 | tf_op jit(solution)/shard_map/eril,jl->erij/dot_general | solution.py:39
  54.8 0.4 convolution_add_fusion.11
  55.3 2.2 %fusion.7 = bf16[4,1,2,128,128]{4,3,2,0,1:T(8,128)(2,1)} fusion(f32[4,2,128,128]{3,2,1,0:T(8,128)} %convolution_add_fusion.16, bf16[4,6,2,128,128]{4,3,2,1,0:T(8,128)(2,1)S(1)} %constant_dynamic-update-slice_fusion, s32[]{:T(128)S(6)} %select_n.66, bf16[2,6,2,128,128]{4,3,2,1,0:T(8,128)(2,1)S(1)} %copy-done), kind=kOutput, calls=%fused_computation.52 | convolution fusion | flops 67502080 | bytes 1114116 | tf_op jit(solution)/shard_map/eril,jl->erij/dot_general | solution.py:39
  57.5 1.1 %fusion.6 = bf16[4,1,2,128,128]{4,3,2,0,1:T(8,128)(2,1)} fusion(f32[4,2,128,128]{3,2,1,0:T(8,128)S(1)} %convolution_add_fusion.11, bf16[4,6,2,128,128]{4,3,2,1,0:T(8,128)(2,1)S(1)} %constant_dynamic-update-slice_fusion, s32[]{:T(128)S(6)} %select_n.66, bf16[2,6,2,128,128]{4,3,2,1,0:T(8,128)(2,1)S(1)} %copy-done), kind=kOutput, calls=%fused_computation.51 | convolution fusion | flops 67502080 | bytes 1114116 | tf_op jit(solution)/shard_map/eril,jl->erij/dot_general | solution.py:39
  58.6 1.1 %maximum_bitcast_fusion = (bf16[4,1,2,2,128,128]{5,4,3,0,2,1:T(8,128)(2,1)S(1)}, bf16[4,1,2,2,128,128]{5,4,3,0,2,1:T(8,128)(2,1)S(1)}) fusion(bf16[4,1,2,128,128]{4,3,2,0,1:T(8,128)(2,1)} %fusion.6, bf16[4,1,2,128,128]{4,3,2,0,1:T(8,128)(2,1)} %fusion.7, bf16[4,1,2,128,128]{4,3,2,0,1:T(8,128)(2,1)S(1)} %copy-done.3, bf16[4,1,2,128,128]{4,3,2,0,1:T(8,128)(2,1)S(1)} %copy-done.2), kind=kLoop, calls=%fused_computation.84 | loop fusion | flops 524288 | bytes 2097152 | tf_op jit(solution)/shard_map/stack | solution.py:44
  59.7 0.0 copy-start.4
  59.7 0.0 copy-start.5
  59.7 0.1 pad_maximum_fusion.1
  59.8 4.0 %collective-permute-start.2 = (bf16[4,2,2,2,128,128]{5,4,3,0,2,1:T(8,128)(2,1)S(1)}, bf16[4,2,2,2,128,128]{5,4,3,0,2,1:T(8,128)(2,1)S(1)}, u32[]{:S(2)}, u32[]{:S(2)}) collective-permute-start(bf16[4,2,2,2,128,128]{5,4,3,0,2,1:T(8,128)(2,1)S(1)} %pad_maximum_fusion.1), channel_id=1, source_target_pairs={{0,4},{4,8},{8,12},{12,16},{16,20},{20,24},{24,28},{1,5},{5,9},{9,... | collective-permute-start | bytes 3145736 | tf_op jit(solution)/shard_map/ppermute | solution.py:17
  63.8 1.9 %collective-permute-start.3 = (bf16[4,2,2,2,128,128]{5,4,3,0,2,1:T(8,128)(2,1)S(1)}, bf16[4,2,2,2,128,128]{5,4,3,0,2,1:T(8,128)(2,1)}, u32[]{:S(2)}, u32[]{:S(2)}) collective-permute-start(bf16[4,2,2,2,128,128]{5,4,3,0,2,1:T(8,128)(2,1)S(1)} %pad_maximum_fusion.1), channel_id=1, source_target_pairs={{4,0},{8,4},{12,8},{16,12},{20,16},{24,20},{28,24},{5,1},{9,5},{13... | collective-permute-start | bytes 3145736 | tf_op jit(solution)/shard_map/ppermute | solution.py:18
  65.7 0.0 copy-done.4
  65.7 0.6 fusion.280
  71.4 0.6 fusion.279
  73.4 2.1 %collective-permute-done.2 = bf16[4,2,2,2,128,128]{5,4,3,0,2,1:T(8,128)(2,1)S(1)} collective-permute-done((bf16[4,2,2,2,128,128]{5,4,3,0,2,1:T(8,128)(2,1)S(1)}, bf16[4,2,2,2,128,128]{5,4,3,0,2,1:T(8,128)(2,1)S(1)}, u32[]{:S(2)}, u32[]{:S(2)}) %collective-permute-start.2) | collective-permute-done | bytes 1048608 | tf_op jit(solution)/shard_map/ppermute | solution.py:17
  75.5 13.0 %collective-permute-done.3 = bf16[4,2,2,2,128,128]{5,4,3,0,2,1:T(8,128)(2,1)} collective-permute-done((bf16[4,2,2,2,128,128]{5,4,3,0,2,1:T(8,128)(2,1)S(1)}, bf16[4,2,2,2,128,128]{5,4,3,0,2,1:T(8,128)(2,1)}, u32[]{:S(2)}, u32[]{:S(2)}) %collective-permute-start.3) | collective-permute-done | bytes 1048608 | tf_op jit(solution)/shard_map/ppermute | solution.py:18
  88.5 1.4 %pad_maximum_fusion = bf16[12,2,2,2,128,128]{5,4,3,0,2,1:T(8,128)(2,1)S(1)} fusion(bf16[4,2,2,2,128,128]{5,4,3,0,2,1:T(8,128)(2,1)} %collective-permute-done.3, bf16[4,1,2,2,128,128]{5,4,3,0,2,1:T(8,128)(2,1)S(1)} %get-tuple-element.24, bf16[4,1,2,2,128,128]{5,4,3,0,2,1:T(8,128)(2,1)S(1)} %get-tuple-element.23, ...), kind=kLoop, calls=%fused_computation | loop fusion | flops 4718592 | bytes 6291456 | tf_op jit(solution)/shard_map/concatenate | solution.py:19
  89.9 0.4 fusion.277
  90.3 1.7 %fusion.36 = bf16[4,2,2,128,128]{4,3,2,0,1:T(8,128)(2,1)S(1)} fusion(bf16[12,2,1,2,128,128]{5,4,3,0,2,1:T(8,128)(2,1)S(1)} %get-tuple-element.6, s32[]{:T(128)S(6)} %select_n.76, f32[]{:T(128)} %bitcast.131, s32[]{:T(128)S(6)} %select_n.75, f32[]{:T(128)S(6)} %add.212, bf16[12,2,1,2,128,128]{5,4,3,0,2,1:T(8,128)(2,1)S(1)} %get-tuple-element.5, ...), kind=kLoop, calls=%fused_computation.83 | loop fusion | flops 3145728 | bytes 2621472 | tf_op jit(solution)/shard_map/convert_element_type | solution.py:67
  92.1 0.8 copy.6
  (9 shorter events, 0.1 us)
Async XLA Ops:
  0.0 29.3 %collective-permute-start = (bf16[4,2,2,128,128]{4,3,2,1,0:T(8,128)(2,1)}, bf16[4,2,2,128,128]{4,3,2,1,0:T(8,128)(2,1)S(1)}, u32[]{:S(2)}, u32[]{:S(2)}) collective-permute-start(bf16[4,2,2,128,128]{4,3,2,1,0:T(8,128)(2,1)} %param.5), channel_id=1, source_target_pairs={{0,1},{1,2},{2,3},{4,5},{5,6},{6,7},{8,9},{9,10},{10,11},{12,13},{... | collective-permute-start | bytes 1572872 | tf_op jit(solution)/shard_map/ppermute | solution.py:17
  4.0 26.5 %collective-permute-start.1 = (bf16[4,2,2,128,128]{4,3,2,1,0:T(8,128)(2,1)}, bf16[4,2,2,128,128]{4,3,2,1,0:T(8,128)(2,1)S(1)}, u32[]{:S(2)}, u32[]{:S(2)}) collective-permute-start(bf16[4,2,2,128,128]{4,3,2,1,0:T(8,128)(2,1)} %param.5), channel_id=1, source_target_pairs={{1,0},{2,1},{3,2},{5,4},{6,5},{7,6},{9,8},{10,9},{11,10},{13,12},{... | collective-permute-start | bytes 1572872 | tf_op jit(solution)/shard_map/ppermute | solution.py:18
  29.3 1.4 %copy-start = (bf16[2,6,2,128,128]{4,3,2,1,0:T(8,128)(2,1)S(1)}, bf16[2,6,2,128,128]{4,3,2,1,0:T(8,128)(2,1)}, u32[]{:S(2)}) copy-start(bf16[2,6,2,128,128]{4,3,2,1,0:T(8,128)(2,1)} %param.6) | copy-start | bytes 2359300
  43.3 3.3 %copy-start.1 = (f32[4,2,128,128]{3,2,1,0:T(8,128)S(1)}, f32[4,2,128,128]{3,2,1,0:T(8,128)}, u32[]{:S(2)}) copy-start(f32[4,2,128,128]{3,2,1,0:T(8,128)} %fusion.9) | copy-start | bytes 1572868
  55.2 3.3 %copy-start.2 = (bf16[4,1,2,128,128]{4,3,2,0,1:T(8,128)(2,1)S(1)}, bf16[4,1,2,128,128]{4,3,2,0,1:T(8,128)(2,1)}, u32[]{:S(2)}) copy-start(bf16[4,1,2,128,128]{4,3,2,0,1:T(8,128)(2,1)} %fusion.5) | copy-start | bytes 786436
  55.2 3.3 %copy-start.3 = (bf16[4,1,2,128,128]{4,3,2,0,1:T(8,128)(2,1)S(1)}, bf16[4,1,2,128,128]{4,3,2,0,1:T(8,128)(2,1)}, u32[]{:S(2)}) copy-start(bf16[4,1,2,128,128]{4,3,2,0,1:T(8,128)(2,1)} %fusion.4) | copy-start | bytes 786436
  59.7 6.0 %copy-start.4 = (s32[2]{0:T(128)S(1)}, s32[2]{0:T(128)}, u32[]{:S(2)}) copy-start(s32[2]{0:T(128)} %param.8) | copy-start | bytes 28
  59.7 11.7 %copy-start.5 = (f32[2]{0:T(128)S(1)}, f32[2]{0:T(128)}, u32[]{:S(2)}) copy-start(f32[2]{0:T(128)} %param.9) | copy-start | bytes 28
  59.8 15.7 %collective-permute-start.2 = (bf16[4,2,2,2,128,128]{5,4,3,0,2,1:T(8,128)(2,1)S(1)}, bf16[4,2,2,2,128,128]{5,4,3,0,2,1:T(8,128)(2,1)S(1)}, u32[]{:S(2)}, u32[]{:S(2)}) collective-permute-start(bf16[4,2,2,2,128,128]{5,4,3,0,2,1:T(8,128)(2,1)S(1)} %pad_maximum_fusion.1), channel_id=1, source_target_pairs={{0,4},{4,8},{8,12},{12,16},{16,20},{20,24},{24,28},{1,5},{5,9},{9,... | collective-permute-start | bytes 3145736 | tf_op jit(solution)/shard_map/ppermute | solution.py:17
  63.8 24.7 %collective-permute-start.3 = (bf16[4,2,2,2,128,128]{5,4,3,0,2,1:T(8,128)(2,1)S(1)}, bf16[4,2,2,2,128,128]{5,4,3,0,2,1:T(8,128)(2,1)}, u32[]{:S(2)}, u32[]{:S(2)}) collective-permute-start(bf16[4,2,2,2,128,128]{5,4,3,0,2,1:T(8,128)(2,1)S(1)} %pad_maximum_fusion.1), channel_id=1, source_target_pairs={{4,0},{8,4},{12,8},{16,12},{20,16},{24,20},{28,24},{5,1},{9,5},{13... | collective-permute-start | bytes 3145736 | tf_op jit(solution)/shard_map/ppermute | solution.py:18
where the time goes:
time: 94.2 us; the launch traced here: 92.9 us
  between operations  29.2 us (31%)
  matrix products  27.8 us (30%)
  waiting for transfers between devices  15.1 us (16%)
  starting transfers between devices  11.2 us (12%)
  other arithmetic  5.05 us (5%)
  local copies, waits for them, and re-layouts  4.49 us (5%)
    dot_general x24, matrix products, mode_products(): jnp.einsum('eril,jl->erij', half_product, matrix, preferred_element_type=...  27.8 us
    ppermute x2, waiting for transfers between devices, with_halo(): after = lax.ppermute(first, axis, down)  13 us
    ppermute x2, starting transfers between devices, with_halo(): before = lax.ppermute(last, axis, up)  8 us
    ppermute x2, starting transfers between devices, with_halo(): after = lax.ppermute(first, axis, down)  3.21 us
    ppermute x2, waiting for transfers between devices, with_halo(): before = lax.ppermute(last, axis, up)  2.09 us
  transfers between devices with their start and end apart: 4, of which 2 were waited for; matrix products, arithmetic and copies ran while one was open for 4% of the time, Pallas kernels for 0%

commit v1 on v0

v1 whole, which is shorter than its diff:
```python
import functools

import jax
import jax.numpy as jnp
from jax import lax
from jax.experimental import pallas as pl
from jax.experimental.pallas import tpu as pltpu
from jax.sharding import PartitionSpec as P

WID = 4
HALO = 2
MESH = pl.DeviceIdType.MESH


def energy_order(count):
    order = []
    for low in range((count + 1) // 2):
        order.append(low)
        if count - 1 - low != low:
            order.append(count - 1 - low)
    return order


def kernel(sizes, nbr, shifts, occ, green, coupling, out, *scratch):
    energies, atoms, parts, blk, slots, modes, n_energy, n_slab = sizes
    wide = scratch[:energies]
    (coup, prod, low_send, up_send, low_recv, up_recv, own, result,
     coup_sem, local_sem, slab_send, slab_recv, en_send, en_recv, out_sem) = scratch[energies:]
    me_e = lax.axis_index("energy")
    me_s = lax.axis_index("slab")
    has_prev, has_next = me_e > 0, me_e < n_energy - 1
    has_left, has_right = me_s > 0, me_s < n_slab - 1
    order = energy_order(energies)

    coup_copy = pltpu.make_async_copy(coupling, coup, coup_sem)
    local = [
        pltpu.make_async_copy(green.at[e], wide[e].at[HALO : HALO + atoms], local_sem.at[e])
        for e in range(energies)
    ]
    for e in order:
        local[e].start()
    coup_copy.start()

    barrier = pltpu.get_barrier_semaphore()
    sides = (
        (has_left, {"slab": me_s - 1}),
        (has_right, {"slab": me_s + 1}),
        (has_prev, {"energy": me_e - 1}),
        (has_next, {"energy": me_e + 1}),
    )
    for there, device in sides:
        @pl.when(there)
        def _(device=device):
            pl.semaphore_signal(barrier, inc=1, device_id=device, device_id_type=MESH)
    peers = sum(there.astype(jnp.int32) for there, _ in sides)
    pl.semaphore_wait(barrier, peers)

    def slab_copy(e, direction):
        if direction == 0:
            src, dst, to = green.at[e, atoms - HALO : atoms], wide[e].at[0:HALO], me_s + 1
        else:
            src, dst, to = green.at[e, 0:HALO], wide[e].at[HALO + atoms : 2 * HALO + atoms], me_s - 1
        return pltpu.make_async_remote_copy(
            src_ref=src,
            dst_ref=dst,
            send_sem=slab_send.at[direction, e],
            recv_sem=slab_recv.at[direction, e],
            device_id={"slab": to},
            device_id_type=MESH,
        )

    for e in order:
        @pl.when(has_right)
        def _(e=e):
            slab_copy(e, 0).start()
        @pl.when(has_left)
        def _(e=e):
            slab_copy(e, 1).start()

    def energy_copy(u, direction):
        if direction == 0:
            src, dst, to = low_send.at[u], low_recv.at[u], me_e + 1
        else:
            src, dst, to = up_send.at[u], up_recv.at[u], me_e - 1
        return pltpu.make_async_remote_copy(
            src_ref=src,
            dst_ref=dst,
            send_sem=en_send.at[direction, u],
            recv_sem=en_recv.at[direction, u],
            device_id={"energy": to},
            device_id_type=MESH,
        )

    @pl.when(jnp.logical_not(has_prev))
    def _():
        low_recv[...] = jnp.zeros_like(low_recv)
    @pl.when(jnp.logical_not(has_next))
    def _():
        up_recv[...] = jnp.zeros_like(up_recv)

    first_atom = me_s * atoms

    def products(e):
        def body(a, carry):
            halves, mats = [], []
            for j in range(slots):
                g = wide[e][jnp.clip(nbr[a, j] - first_atom + HALO, 0, atoms + 2 * HALO - 1)]
                g = jnp.concatenate([g[r] for r in range(parts)], axis=1)
                c = coup[a, j]
                mats.append(c)
                h = jnp.dot(c.reshape(modes * blk, blk), g, preferred_element_type=jnp.float32)
                halves.append(h.astype(jnp.bfloat16))
            for m in range(modes):
                rows = [
                    jnp.concatenate(
                        [h[m * blk : (m + 1) * blk, r * blk : (r + 1) * blk] for h in halves], axis=1
                    )
                    for r in range(parts)
                ]
                lhs = jnp.concatenate(rows, axis=0)
                rhs = jnp.concatenate([c[m] for c in mats], axis=1)
                p = lax.dot_general(lhs, rhs, (((1,), (1,)), ((), ())), preferred_element_type=jnp.float32)
                prod[m, e, a] = p.reshape(parts, blk, blk).astype(jnp.bfloat16)
            return carry

        lax.fori_loop(0, atoms, body, 0)

    def gathered(terms):
        def at(a):
            total = None
            for m, index, weight in terms:
                inside = (index >= 0) & (index < energies)
                safe = jnp.clip(index, 0, energies - 1)
                term = jnp.where(inside, weight, 0.0) * prod[m, safe, a].astype(jnp.float32)
                total = term if total is None else total + term
            return total

        return at

    def store_sum(target, u, terms):
        at = gathered(terms)

        def body(a, carry):
            target[u, a] = at(a).astype(target.dtype)
            return carry

        lax.fori_loop(0, atoms, body, 0)

    done, sent = set(), set()
    for e in order:
        local[e].wait()
        if not done:
            coup_copy.wait()
        @pl.when(has_left)
        def _(e=e):
            slab_copy(e, 0).wait_recv()
        @pl.when(has_right)
        def _(e=e):
            slab_copy(e, 1).wait_recv()
        products(e)
        done.add(e)
        for u in range(WID):
            if ("up", u) not in sent and set(range(u + 1)) <= done:
                sent.add(("up", u))
                @pl.when(has_prev)
                def _(u=u):
                    store_sum(up_send, u, [(m, u - WID + shifts[m], occ[m]) for m in range(modes)])
                    energy_copy(u, 1).start()
        for u in reversed(range(WID)):
            if ("low", u) not in sent and set(range(energies - WID + u, energies)) <= done:
                sent.add(("low", u))
                @pl.when(has_next)
                def _(u=u):
                    store_sum(low_send, u, [(m, energies + u - shifts[m], occ[m] + 1.0) for m in range(modes)])
                    energy_copy(u, 0).start()

    for t in range(energies):
        terms = []
        for m in range(modes):
            terms.append((m, t - shifts[m], occ[m] + 1.0))
            terms.append((m, t + shifts[m], occ[m]))
        store_sum(own, t, terms)

    for t in order:
        low_u = t if t < WID else None
        up_u = t - (energies - WID) if t >= energies - WID else None
        if low_u is not None:
            @pl.when(has_prev)
            def _(u=low_u):
                energy_copy(u, 0).wait_recv()
        if up_u is not None:
            @pl.when(has_next)
            def _(u=up_u):
                energy_copy(u, 1).wait_recv()

        def body(a, carry, t=t, low_u=low_u, up_u=up_u):
            total = own[t, a]
            if low_u is not None:
                total = total + low_recv[low_u, a].astype(jnp.float32)
            if up_u is not None:
                total = total + up_recv[up_u, a].astype(jnp.float32)
            result[t, a] = total.astype(jnp.bfloat16)
            return carry

        lax.fori_loop(0, atoms, body, 0)
        pltpu.make_async_copy(result.at[t], out.at[t], out_sem.at[t]).start()

    for e in order:
        @pl.when(has_right)
        def _(e=e):
            slab_copy(e, 0).wait_send()
        @pl.when(has_left)
        def _(e=e):
            slab_copy(e, 1).wait_send()
    for u in range(WID):
        @pl.when(has_next)
        def _(u=u):
            energy_copy(u, 0).wait_send()
        @pl.when(has_prev)
        def _(u=u):
            energy_copy(u, 1).wait_send()
    for t in order:
        pltpu.make_async_copy(result.at[t], out.at[t], out_sem.at[t]).wait()


def solution(mesh):
    def shards(green, coupling, neighbours, shifts, occupation):
        energies, atoms, parts, blk, _ = green.shape
        slots, modes = coupling.shape[1:3]
        sizes = (energies, atoms, parts, blk, slots, modes, mesh.shape["energy"], mesh.shape["slab"])
        bf16, f32 = jnp.bfloat16, jnp.float32
        smem = pl.BlockSpec(memory_space=pltpu.SMEM)
        hbm = pl.BlockSpec(memory_space=pl.ANY)
        edge = (WID, atoms, parts, blk, blk)
        dma = pltpu.SemaphoreType.DMA
        return pl.pallas_call(
            functools.partial(kernel, sizes),
            out_shape=jax.ShapeDtypeStruct(green.shape, bf16),
            in_specs=[smem, smem, smem, hbm, hbm],
            out_specs=hbm,
            scratch_shapes=[pltpu.VMEM((atoms + 2 * HALO, parts, blk, blk), bf16) for _ in range(energies)]
            + [
                pltpu.VMEM(coupling.shape, bf16),
                pltpu.VMEM((modes, energies, atoms, parts, blk, blk), bf16),
                pltpu.VMEM(edge, bf16),
                pltpu.VMEM(edge, bf16),
                pltpu.VMEM(edge, bf16),
                pltpu.VMEM(edge, bf16),
                pltpu.VMEM(green.shape, f32),
                pltpu.VMEM(green.shape, bf16),
                dma,
                dma((energies,)),
                dma((2, energies)),
                dma((2, energies)),
                dma((2, WID)),
                dma((2, WID)),
                dma((energies,)),
            ],
            compiler_params=pltpu.CompilerParams(collective_id=0, has_side_effects=True),
        )(neighbours, shifts, occupation, green, coupling)

    return jax.shard_map(
        shards,
        mesh=mesh,
        in_specs=(
            P("energy", "slab", None, None, None),
            P("slab", None, None, None, None),
            P("slab", None),
            P(),
            P(),
        ),
        out_specs=P("energy", "slab", None, None, None),
        check_vma=False,
    )
```

time: 94.2 us -> 30.1 us (0.32); the launches traced: 92.9 us -> 29.9 us
  between operations: 29.2 us -> 0.01 us
  Pallas kernels: 0 us -> 28.1 us
  matrix products: 27.8 us -> 0 us
  waiting for transfers between devices: 15.1 us -> 0 us
  starting transfers between devices: 11.2 us -> 0 us
  other arithmetic: 5.05 us -> 0 us
  local copies, waits for them, and re-layouts: 4.49 us -> 1.89 us
    pallas_call x0 -> x1, Pallas kernels: none -> 28.1 us  [shards(): pl.pallas_call(functools.partial(kernel, sizes), out_shape=jax.ShapeDtype...]
    dot_general x24 -> x0, matrix products: 27.8 us -> none  [mode_products(): jnp.einsum('eril,jl->erij', half_product, matrix, preferred_element_type=...]
    ppermute x4 -> x0, waiting for transfers between devices: 15.1 us -> none  [the longest x2 13 us: with_halo(): after = lax.ppermute(first, axis, down)]
    ppermute x4 -> x0, starting transfers between devices: 11.2 us -> none  [the longest x2 8 us: with_halo(): before = lax.ppermute(last, axis, up)]
    slice x4 -> x0, local copies, waits for them, and re-layouts: 2.34 us -> none  [the longest x1 0.69 us: mode_products(): local_index[which_atom, which_slot]]
    convert_element_type x1 -> x0, other arithmetic: 1.72 us -> none  [shards(): return result.astype(jnp.bfloat16)]
    concatenate x1 -> x0, other arithmetic: 1.42 us -> none  [with_halo(): x = jnp.concatenate([before, x, after], axis=dim)]
    another operation x2 -> x0, other arithmetic: 1.22 us -> none  [mode_products(): return jnp.stack(atom_blocks, 1)]
  transfers between devices with their start and end apart: 4 -> 0, of which waited for: 2 -> 0; matrix products, arithmetic and copies ran while one was open for 4% -> 0% of each run, Pallas kernels for 0% -> 0%
where the time goes in v1:
time: 30.1 us; the launch traced here: 29.9 us
  Pallas kernels  28.1 us (93%)
  local copies, waits for them, and re-layouts  1.89 us (6%)
    pallas_call x1, Pallas kernels, shards(): pl.pallas_call(functools.partial(kernel, sizes), out_shape=jax.ShapeDtype...  28.1 us
    unnamed x1, local copies, waits for them, and re-layouts  1.89 us

profile of v1, /device:TPU:1, one launch (start us, length us, event | category | flops | bytes accessed | tf_op | source)
XLA Modules:
  0.0 29.9 jit_solution(11680716619054909140)
XLA Ops:
  0.0 28.1 %shard_map.55 = bf16[4,2,2,128,128]{4,3,2,1,0:T(8,128)(2,1)} custom-call(s32[2,6]{1,0:T(2,128)} %nbr.1, s32[2]{0:T(128)} %shifts.1, f32[2]{0:T(128)} %occ.1, bf16[4,2,2,128,128]{4,3,2,1,0:T(8,128)(2,1)} %green.1, bf16[2,6,2,128,128]{4,3,2,1,0:T(8,128)(2,1)} %coupling.1), custom_call_target="tpu_custom_call" | custom-call | tf_op jit(solution)/shard_map/pallas_call | solution.py:236
  28.1 1.9 %copy.7 = bf16[4,2,2,128,128]{4,3,2,1,0:T(8,128)(2,1)} copy(bf16[4,2,2,128,128]{4,3,2,1,0:T(8,128)(2,1)} %shard_map.55) | data formatting | bytes 1048576

commit v2 on v1

v2 whole, which is shorter than its diff:
```python
import functools

import jax
import jax.numpy as jnp
from jax import lax
from jax.experimental import pallas as pl
from jax.experimental.pallas import tpu as pltpu
from jax.sharding import PartitionSpec as P

WID = 4
HALO = 2
MESH = pl.DeviceIdType.MESH


def energy_order(count):
    order = []
    for low in range((count + 1) // 2):
        order.append(low)
        if count - 1 - low != low:
            order.append(count - 1 - low)
    return order


def kernel(sizes, nbr, shifts, occ, green, coupling, out, *scratch):
    energies, atoms, parts, blk, slots, modes, n_energy, n_slab = sizes
    wide = [scratch[r * energies : (r + 1) * energies] for r in range(parts)]
    (coup, prod, low_send, up_send, low_recv, up_recv, own,
     coup_sem, local_sem, slab_send, slab_recv, en_send, en_recv) = scratch[parts * energies :]
    me_e = lax.axis_index("energy")
    me_s = lax.axis_index("slab")
    has_prev, has_next = me_e > 0, me_e < n_energy - 1
    has_left, has_right = me_s > 0, me_s < n_slab - 1
    order = energy_order(energies)

    coup_copy = pltpu.make_async_copy(coupling, coup, coup_sem)
    local = [
        [
            pltpu.make_async_copy(green.at[e, :, r], wide[r][e].at[HALO : HALO + atoms], local_sem.at[r, e])
            for e in range(energies)
        ]
        for r in range(parts)
    ]
    for r in range(parts):
        for e in order:
            local[r][e].start()
    coup_copy.start()

    barrier = pltpu.get_barrier_semaphore()
    sides = (
        (has_left, {"slab": me_s - 1}),
        (has_right, {"slab": me_s + 1}),
        (has_prev, {"energy": me_e - 1}),
        (has_next, {"energy": me_e + 1}),
    )
    for there, device in sides:
        @pl.when(there)
        def _(device=device):
            pl.semaphore_signal(barrier, inc=1, device_id=device, device_id_type=MESH)
    peers = sum(there.astype(jnp.int32) for there, _ in sides)
    pl.semaphore_wait(barrier, peers)

    def slab_copy(r, e, direction):
        halo = wide[r][e]
        if direction == 0:
            src, dst, to = green.at[e, atoms - HALO : atoms, r], halo.at[0:HALO], me_s + 1
        else:
            src, dst, to = green.at[e, 0:HALO, r], halo.at[HALO + atoms : 2 * HALO + atoms], me_s - 1
        return pltpu.make_async_remote_copy(
            src_ref=src,
            dst_ref=dst,
            send_sem=slab_send.at[direction, r, e],
            recv_sem=slab_recv.at[direction, r, e],
            device_id={"slab": to},
            device_id_type=MESH,
        )

    for r in range(parts):
        for e in order:
            @pl.when(has_right)
            def _(e=e, r=r):
                slab_copy(r, e, 0).start()
            @pl.when(has_left)
            def _(e=e, r=r):
                slab_copy(r, e, 1).start()

    def energy_copy(r, u, direction):
        if direction == 0:
            src, dst, to = low_send.at[r, u], low_recv.at[r, u], me_e + 1
        else:
            src, dst, to = up_send.at[r, u], up_recv.at[r, u], me_e - 1
        return pltpu.make_async_remote_copy(
            src_ref=src,
            dst_ref=dst,
            send_sem=en_send.at[direction, r, u],
            recv_sem=en_recv.at[direction, r, u],
            device_id={"energy": to},
            device_id_type=MESH,
        )

    @pl.when(jnp.logical_not(has_prev))
    def _():
        low_recv[...] = jnp.zeros_like(low_recv)
    @pl.when(jnp.logical_not(has_next))
    def _():
        up_recv[...] = jnp.zeros_like(up_recv)

    first_atom = me_s * atoms

    def products(r, e):
        def body(a, carry):
            halves, mats = [], []
            for j in range(slots):
                g = wide[r][e][jnp.clip(nbr[a, j] - first_atom + HALO, 0, atoms + 2 * HALO - 1)]
                c = coup[a, j]
                mats.append(c)
                h = jnp.dot(c.reshape(modes * blk, blk), g, preferred_element_type=jnp.float32)
                halves.append(h.astype(jnp.bfloat16))
            for m in range(modes):
                lhs = jnp.concatenate([h[m * blk : (m + 1) * blk] for h in halves], axis=1)
                rhs = jnp.concatenate([c[m] for c in mats], axis=1)
                p = lax.dot_general(lhs, rhs, (((1,), (1,)), ((), ())), preferred_element_type=jnp.float32)
                prod[m, r, e, a] = p.astype(jnp.bfloat16)
            return carry

        lax.fori_loop(0, atoms, body, 0)

    def store_sum(target, r, u, terms):
        def body(a, carry):
            total = None
            for m, index, weight in terms:
                inside = (index >= 0) & (index < energies)
                safe = jnp.clip(index, 0, energies - 1)
                term = jnp.where(inside, weight, 0.0) * prod[m, r, safe, a].astype(jnp.float32)
                total = term if total is None else total + term
            target[r, u, a] = total.astype(target.dtype)
            return carry

        lax.fori_loop(0, atoms, body, 0)

    for r in range(parts):
        done, sent = set(), set()
        for e in order:
            local[r][e].wait()
            if r == 0 and not done:
                coup_copy.wait()
            @pl.when(has_left)
            def _(e=e, r=r):
                slab_copy(r, e, 0).wait_recv()
            @pl.when(has_right)
            def _(e=e, r=r):
                slab_copy(r, e, 1).wait_recv()
            products(r, e)
            done.add(e)
            for u in range(WID):
                if ("up", u) not in sent and set(range(u + 1)) <= done:
                    sent.add(("up", u))
                    @pl.when(has_prev)
                    def _(u=u, r=r):
                        store_sum(up_send, r, u, [(m, u - WID + shifts[m], occ[m]) for m in range(modes)])
                        energy_copy(r, u, 1).start()
            for u in reversed(range(WID)):
                if ("low", u) not in sent and set(range(energies - WID + u, energies)) <= done:
                    sent.add(("low", u))
                    @pl.when(has_next)
                    def _(u=u, r=r):
                        store_sum(
                            low_send, r, u, [(m, energies + u - shifts[m], occ[m] + 1.0) for m in range(modes)]
                        )
                        energy_copy(r, u, 0).start()

    for r in range(parts):
        for t in range(energies):
            terms = []
            for m in range(modes):
                terms.append((m, t - shifts[m], occ[m] + 1.0))
                terms.append((m, t + shifts[m], occ[m]))
            store_sum(own, r, t, terms)

    for r in range(parts):
        for t in order:
            low_u = t if t < WID else None
            up_u = t - (energies - WID) if t >= energies - WID else None
            if low_u is not None:
                @pl.when(has_prev)
                def _(u=low_u, r=r):
                    energy_copy(r, u, 0).wait_recv()
            if up_u is not None:
                @pl.when(has_next)
                def _(u=up_u, r=r):
                    energy_copy(r, u, 1).wait_recv()

            def body(a, carry, t=t, r=r, low_u=low_u, up_u=up_u):
                total = own[r, t, a]
                if low_u is not None:
                    total = total + low_recv[r, low_u, a].astype(jnp.float32)
                if up_u is not None:
                    total = total + up_recv[r, up_u, a].astype(jnp.float32)
                out[t, a, r] = total.astype(jnp.bfloat16)
                return carry

            lax.fori_loop(0, atoms, body, 0)

    for r in range(parts):
        for e in order:
            @pl.when(has_right)
            def _(e=e, r=r):
                slab_copy(r, e, 0).wait_send()
            @pl.when(has_left)
            def _(e=e, r=r):
                slab_copy(r, e, 1).wait_send()
        for u in range(WID):
            @pl.when(has_next)
            def _(u=u, r=r):
                energy_copy(r, u, 0).wait_send()
            @pl.when(has_prev)
            def _(u=u, r=r):
                energy_copy(r, u, 1).wait_send()


def solution(mesh):
    def shards(green, coupling, neighbours, shifts, occupation):
        energies, atoms, parts, blk, _ = green.shape
        slots, modes = coupling.shape[1:3]
        sizes = (energies, atoms, parts, blk, slots, modes, mesh.shape["energy"], mesh.shape["slab"])
        bf16, f32 = jnp.bfloat16, jnp.float32
        smem = pl.BlockSpec(memory_space=pltpu.SMEM)
        hbm = pl.BlockSpec(memory_space=pl.ANY)
        edge = (parts, WID, atoms, blk, blk)
        dma = pltpu.SemaphoreType.DMA
        return pl.pallas_call(
            functools.partial(kernel, sizes),
            out_shape=jax.ShapeDtypeStruct(green.shape, bf16),
            in_specs=[smem, smem, smem, hbm, hbm],
            out_specs=pl.BlockSpec(memory_space=pltpu.VMEM),
            scratch_shapes=[pltpu.VMEM((atoms + 2 * HALO, blk, blk), bf16) for _ in range(parts * energies)]
            + [
                pltpu.VMEM(coupling.shape, bf16),
                pltpu.VMEM((modes, parts, energies, atoms, blk, blk), bf16),
                pltpu.VMEM(edge, bf16),
                pltpu.VMEM(edge, bf16),
                pltpu.VMEM(edge, bf16),
                pltpu.VMEM(edge, bf16),
                pltpu.VMEM((parts, energies, atoms, blk, blk), f32),
                dma,
                dma((parts, energies)),
                dma((2, parts, energies)),
                dma((2, parts, energies)),
                dma((2, parts, WID)),
                dma((2, parts, WID)),
            ],
            compiler_params=pltpu.CompilerParams(collective_id=0, has_side_effects=True),
        )(neighbours, shifts, occupation, green, coupling)

    return jax.shard_map(
        shards,
        mesh=mesh,
        in_specs=(
            P("energy", "slab", None, None, None),
            P("slab", None, None, None, None),
            P("slab", None),
            P(),
            P(),
        ),
        out_specs=P("energy", "slab", None, None, None),
        check_vma=False,
    )
```

time: 30.1 us -> 27.7 us (0.920)
  Pallas kernels: 28.1 us -> 25.6 us
    pallas_call x1, Pallas kernels: 28.1 us -> 25.6 us  [shards(): pl.pallas_call(functools.partial(kernel, sizes), out_shape=jax.ShapeDtype...]
where the time goes in v2:
time: 27.7 us; the launch traced here: 27.5 us
  Pallas kernels  25.6 us (92%)
  local copies, waits for them, and re-layouts  1.89 us (7%)
    pallas_call x1, Pallas kernels, shards(): pl.pallas_call(functools.partial(kernel, sizes), out_shape=jax.ShapeDtype...  25.6 us
    unnamed x1, local copies, waits for them, and re-layouts  1.89 us

profile of v2, /device:TPU:1, one launch (start us, length us, event | category | flops | bytes accessed | tf_op | source)
XLA Modules:
  0.0 27.5 jit_solution(4480403121091131748)
XLA Ops:
  0.0 25.6 %shard_map.55 = bf16[4,2,2,128,128]{4,3,2,1,0:T(8,128)(2,1)} custom-call(s32[2,6]{1,0:T(2,128)} %nbr.1, s32[2]{0:T(128)} %shifts.1, f32[2]{0:T(128)} %occ.1, bf16[4,2,2,128,128]{4,3,2,1,0:T(8,128)(2,1)} %green.1, bf16[2,6,2,128,128]{4,3,2,1,0:T(8,128)(2,1)} %coupling.1), custom_call_target="tpu_custom_call" | custom-call | tf_op jit(solution)/shard_map/pallas_call | solution.py:230
  25.6 1.9 %copy.7 = bf16[4,2,2,128,128]{4,3,2,1,0:T(8,128)(2,1)} copy(bf16[4,2,2,128,128]{4,3,2,1,0:T(8,128)(2,1)} %shard_map.55) | data formatting | bytes 1048576

commit v3 on v2

--- a/solution.py
+++ b/solution.py
@@ -21,17 +21,23 @@
     return order
 
 
-def kernel(sizes, nbr, shifts, occ, green, coupling, out, *scratch):
+def kernel(sizes, nbr_hbm, shifts_hbm, occ_hbm, green, coupling, out, *scratch):
     energies, atoms, parts, blk, slots, modes, n_energy, n_slab = sizes
     wide = [scratch[r * energies : (r + 1) * energies] for r in range(parts)]
-    (coup, prod, low_send, up_send, low_recv, up_recv, own,
-     coup_sem, local_sem, slab_send, slab_recv, en_send, en_recv) = scratch[parts * energies :]
+    (coup, prod, low_send, up_send, low_recv, up_recv, own, nbr, shifts, occ,
+     coup_sem, local_sem, slab_send, slab_recv, en_send, en_recv, small_sem) = scratch[parts * energies :]
     me_e = lax.axis_index("energy")
     me_s = lax.axis_index("slab")
     has_prev, has_next = me_e > 0, me_e < n_energy - 1
     has_left, has_right = me_s > 0, me_s < n_slab - 1
     order = energy_order(energies)
 
+    small = [
+        pltpu.make_async_copy(src, dst, small_sem.at[k])
+        for k, (src, dst) in enumerate(((nbr_hbm, nbr), (shifts_hbm, shifts), (occ_hbm, occ)))
+    ]
+    for copy in small:
+        copy.start()
     coup_copy = pltpu.make_async_copy(coupling, coup, coup_sem)
     local = [
         [
@@ -143,6 +149,8 @@
             local[r][e].wait()
             if r == 0 and not done:
                 coup_copy.wait()
+                for copy in small:
+                    copy.wait()
             @pl.when(has_left)
             def _(e=e, r=r):
                 slab_copy(r, e, 0).wait_recv()
@@ -223,14 +231,13 @@
         slots, modes = coupling.shape[1:3]
         sizes = (energies, atoms, parts, blk, slots, modes, mesh.shape["energy"], mesh.shape["slab"])
         bf16, f32 = jnp.bfloat16, jnp.float32
-        smem = pl.BlockSpec(memory_space=pltpu.SMEM)
-        hbm = pl.BlockSpec(memory_space=pl.ANY)
+        hbm = pl.BlockSpec(memory_space=pltpu.HBM)
         edge = (parts, WID, atoms, blk, blk)
         dma = pltpu.SemaphoreType.DMA
         return pl.pallas_call(
             functools.partial(kernel, sizes),
-            out_shape=jax.ShapeDtypeStruct(green.shape, bf16),
-            in_specs=[smem, smem, smem, hbm, hbm],
+            out_shape=pltpu.VMEM(green.shape, bf16),
+            in_specs=[hbm] * 5,
             out_specs=pl.BlockSpec(memory_space=pltpu.VMEM),
             scratch_shapes=[pltpu.VMEM((atoms + 2 * HALO, blk, blk), bf16) for _ in range(parts * energies)]
             + [
@@ -241,12 +248,16 @@
                 pltpu.VMEM(edge, bf16),
                 pltpu.VMEM(edge, bf16),
                 pltpu.VMEM((parts, energies, atoms, blk, blk), f32),
+                pltpu.SMEM((atoms, slots), jnp.int32),
+                pltpu.SMEM((modes,), jnp.int32),
+                pltpu.SMEM((modes,), f32),
                 dma,
                 dma((parts, energies)),
                 dma((2, parts, energies)),
                 dma((2, parts, energies)),
                 dma((2, parts, WID)),
                 dma((2, parts, WID)),
+                dma((3,)),
             ],
             compiler_params=pltpu.CompilerParams(collective_id=0, has_side_effects=True),
         )(neighbours, shifts, occupation, green, coupling)

time: 27.7 us -> 25.1 us (0.906)
  Pallas kernels: 25.6 us -> 24.1 us
  local copies, waits for them, and re-layouts: 1.89 us -> 0.8 us
    pallas_call x1, Pallas kernels: 25.6 us -> 24.1 us  [shards(): pl.pallas_call(functools.partial(kernel, sizes), out_shape=pltpu.VMEM(gre...]
    unnamed x1, local copies, waits for them, and re-layouts: 1.89 us -> 0.8 us
where the time goes in v3:
time: 25.1 us; the launch traced here: 24.9 us
  Pallas kernels  24.1 us (96%)
  local copies, waits for them, and re-layouts  0.8 us (3%)
    pallas_call x1, Pallas kernels, shards(): pl.pallas_call(functools.partial(kernel, sizes), out_shape=pltpu.VMEM(gre...  24.1 us
    unnamed x1, local copies, waits for them, and re-layouts  0.8 us

profile of v3, /device:TPU:1, one launch (start us, length us, event | category | flops | bytes accessed | tf_op | source)
XLA Modules:
  0.0 24.9 jit_solution(18166114335589884685)
XLA Ops:
  0.0 24.1 %shard_map.55 = bf16[4,2,2,128,128]{4,3,2,1,0:T(8,128)(2,1)S(1)} custom-call(s32[2,6]{1,0:T(2,128)} %nbr_hbm.1, s32[2]{0:T(128)} %shifts_hbm.1, f32[2]{0:T(128)} %occ_hbm.1, bf16[4,2,2,128,128]{4,3,2,1,0:T(8,128)(2,1)} %green.1, bf16[2,6,2,128,128]{4,3,2,1,0:T(8,128)(2,1)} %coupling.1), custom_call_target="tpu_custom_call" | custom-call | tf_op jit(solution)/shard_map/pallas_call | solution.py:237
  24.1 0.8 %copy.7 = bf16[4,2,2,128,128]{4,3,2,1,0:T(8,128)(2,1)} copy(bf16[4,2,2,128,128]{4,3,2,1,0:T(8,128)(2,1)S(1)} %shard_map.55) | data formatting | bytes 1048576

commit v4 on v3

--- a/solution.py
+++ b/solution.py
@@ -185,7 +185,7 @@
             store_sum(own, r, t, terms)
 
     for r in range(parts):
-        for t in order:
+        for t in reversed(order):
             low_u = t if t < WID else None
             up_u = t - (energies - WID) if t >= energies - WID else None
             if low_u is not None:

time: 25.1 us -> 25 us (level)
  no operation moved by 1% of the time
where the time goes in v4:
time: 25 us; the launch traced here: 24.9 us
  Pallas kernels  24.1 us (96%)
  local copies, waits for them, and re-layouts  0.8 us (3%)
    pallas_call x1, Pallas kernels, shards(): pl.pallas_call(functools.partial(kernel, sizes), out_shape=pltpu.VMEM(gre...  24.1 us
    unnamed x1, local copies, waits for them, and re-layouts  0.8 us

profile of v4, /device:TPU:1, one launch (start us, length us, event | category | flops | bytes accessed | tf_op | source)
XLA Modules:
  0.0 24.9 jit_solution(11921506256849054737)
XLA Ops:
  0.0 24.1 %shard_map.55 = bf16[4,2,2,128,128]{4,3,2,1,0:T(8,128)(2,1)S(1)} custom-call(s32[2,6]{1,0:T(2,128)} %nbr_hbm.1, s32[2]{0:T(128)} %shifts_hbm.1, f32[2]{0:T(128)} %occ_hbm.1, bf16[4,2,2,128,128]{4,3,2,1,0:T(8,128)(2,1)} %green.1, bf16[2,6,2,128,128]{4,3,2,1,0:T(8,128)(2,1)} %coupling.1), custom_call_target="tpu_custom_call" | custom-call | tf_op jit(solution)/shard_map/pallas_call | solution.py:237
  24.1 0.8 %copy.7 = bf16[4,2,2,128,128]{4,3,2,1,0:T(8,128)(2,1)} copy(bf16[4,2,2,128,128]{4,3,2,1,0:T(8,128)(2,1)S(1)} %shard_map.55) | data formatting | bytes 1048576
